TPU v7x, 32 devices: a whole 2x2x4 slice. The times are simulated.
32 devices in a mesh: groups: 2 (over x), seq: 8 (over z, y), head: 2 (over core).
Axes of the slice: x: 2, y: 2, z: 4, core: 2. Of those that a mesh axis runs over, the one named last changes fastest.
Arguments:
- query_proj: bfloat16 [4096, 2048], P(('groups', 'seq'), 'head'), parts along dimension 0, may hold values from -6 to 6
- key_proj: bfloat16 [4096, 2048], P(('groups', 'seq'), 'head'), parts along dimension 0, may hold values from -6 to 6
- value_proj: bfloat16 [4096, 2048], P(('groups', 'seq'), 'head'), parts along dimension 0, may hold values from -6 to 6
- segment_ids: int32 [4096], P(('groups', 'seq')), parts along dimension 0, may hold values from 0 to 5, never falling along the last dimension, each value on 1 to 682 neighbouring positions
- feature_map: bfloat16 [16, 128, 256], P('head'), may hold values from -0.5 to 0.5
- head_gain: float32 [2048], P('head'), may hold values from 0.1 to 1.9
- residual: bfloat16 [4096, 2048], P(('groups', 'seq', 'head')), parts along dimension 0, may hold values from -6 to 6
- out_weight: bfloat16 [2048, 2048], P('head'), may hold values from -0.125 to 0.125
- norm_gain: float32 [2048], replicated, may hold values from 0.1 to 1.9
- router: bfloat16 [2048, 16], replicated, may hold values from -0.125 to 0.125
- w_gate: bfloat16 [16, 2048, 1024], P(('seq', 'head')), may hold values from -0.125 to 0.125
- w_up: bfloat16 [16, 2048, 1024], P(('seq', 'head')), may hold values from -0.125 to 0.125
- w_down: bfloat16 [16, 1024, 2048], P(('seq', 'head')), may hold values from -0.1875 to 0.1875
- expert_ids: int32 [4096, 8], P(('groups', 'seq', 'head')), parts along dimension 0, may hold values from 0 to 15, all different within a row; in each aligned block of 128 rows (0 to 127, 128 to 255, ...) at most 80 rows name the same one
Outputs:
- hidden: bfloat16 [4096, 2048], P(('groups', 'seq', 'head')), parts along dimension 0
- expert_sum: bfloat16 [4096, 2048], P(('groups', 'seq', 'head')), parts along dimension 0
There are 2 independent parts, one for each index of `groups`. A program takes and returns all parts, laid end to end along the dimension named above; an argument that names none is the same for every part. Nothing has to cross between parts.
Inputs may be any that keep to these rules, and one draw needn't show every extreme that they name: `segment_ids`: segment ids never fall; every segment has 1 to 682 tokens, one exactly 682. `expert_ids`: A token's 8 experts differ. In the 128 rows of one device (aligned blocks of rows) no expert is named more than 80 times, and in some such block some expert is named exactly 80 times.
All inputs are finite; a program needn't handle non-finite values.
Results may differ from a plain program's by a relative error of at most 0.011.
Values may be sent and summed in bfloat16 or wider, within the bound.
A program may use at most 128 MiB of HBM per device.

v0:
```python
import jax
import jax.numpy as jnp
from jax import lax
from jax.sharding import PartitionSpec as P


def carried_in(last_seg, local_state, token_count):
    place = lax.axis_index("seq")
    blocks = lax.axis_size("seq")
    longest = token_count * blocks // 3
    reach = min(blocks - 1, max(1, (longest - 2) // token_count + 1))
    last_all = lax.all_gather(last_seg, "seq")

    def last_of(back):
        index = place - back
        return jnp.where(index >= 0, last_all[jnp.maximum(index, 0)], -1 - back)

    before = last_of(1)
    carried = None
    window = local_state
    span = 1
    covered = 0
    while covered < reach:
        shifted = lax.ppermute(
            window.astype(jnp.bfloat16), "seq", [(i, i + span) for i in range(blocks - span)]
        ).astype(jnp.float32)
        if carried is None:
            carried = shifted
        else:
            carried = carried + jnp.where(last_of(span) == before, shifted, 0.0)
        covered += span
        if covered < reach:
            window = window + jnp.where(last_of(span) == last_seg, shifted, 0.0)
        span *= 2
    return (before, carried)


def features_of(inputs, feature_map, head_count, head_dim):
    grouped = inputs.reshape(inputs.shape[0], head_count, head_dim)
    projected = jnp.einsum("thd,hdf->thf", grouped, feature_map, preferred_element_type=jnp.float32)
    return (jax.nn.elu(projected) + 1.0).astype(jnp.bfloat16)


def run_expert(rows, gate, w_gate, w_up, w_down):
    gate_pre = jnp.dot(rows, w_gate, preferred_element_type=jnp.float32)
    up_pre = jnp.dot(rows, w_up, preferred_element_type=jnp.float32)
    activated = (jax.nn.silu(gate_pre) * up_pre).astype(jnp.bfloat16)
    answer = jnp.dot(activated, w_down, preferred_element_type=jnp.float32)
    return answer * gate[:, None]


def shards(
    query_proj,
    key_proj,
    value_proj,
    segment_ids,
    feature_map,
    head_gain,
    residual,
    out_weight,
    norm_gain,
    router,
    w_gate,
    w_up,
    w_down,
    expert_ids,
):
    token_count = query_proj.shape[0]
    head_count = feature_map.shape[0]
    head_dim = feature_map.shape[1]
    query_feat = features_of(query_proj, feature_map, head_count, head_dim)
    key_feat = features_of(key_proj, feature_map, head_count, head_dim)
    values = value_proj.reshape(token_count, head_count, head_dim)
    last_seg = segment_ids[token_count - 1]
    tail_mask = (segment_ids == last_seg).astype(jnp.bfloat16)
    local_state = jnp.einsum(
        "thf,thd->hfd",
        key_feat * tail_mask[:, None, None],
        values,
        preferred_element_type=jnp.float32,
    )
    seg_before, state_before = carried_in(last_seg, local_state, token_count)
    scores = jnp.einsum("thf,shf->hts", query_feat, key_feat, preferred_element_type=jnp.float32)
    positions = lax.iota(jnp.int32, token_count)
    allowed = (positions[None, :] <= positions[:, None]) & (
        segment_ids[None, :] == segment_ids[:, None]
    )
    block_weights = jnp.where(allowed[None], scores, 0.0).astype(jnp.bfloat16)
    within = jnp.einsum("hts,shd->thd", block_weights, values, preferred_element_type=jnp.float32)
    carried = jnp.einsum(
        "thf,hfd->thd",
        query_feat,
        state_before.astype(jnp.bfloat16),
        preferred_element_type=jnp.float32,
    )
    carry_mask = (segment_ids == seg_before).astype(jnp.float32)
    mixed = within + carry_mask[:, None, None] * carried
    scale = lax.rsqrt(jnp.mean(mixed * mixed, axis=2, keepdims=True) + 1e-06)
    attn_heads = (
        (mixed * scale * head_gain.reshape(head_count, head_dim))
        .reshape(token_count, head_count * head_dim)
        .astype(jnp.bfloat16)
    )
    attn_rows = lax.all_to_all(attn_heads, "head", split_axis=0, concat_axis=1, tiled=True)
    projected = jnp.dot(
        attn_rows,
        lax.all_gather(out_weight, "head", axis=0, tiled=True),
        preferred_element_type=jnp.float32,
    )
    hidden = (residual.astype(jnp.float32) + projected).astype(jnp.bfloat16)
    hidden_f = hidden.astype(jnp.float32)
    normed = (
        hidden_f
        * lax.rsqrt(jnp.mean(hidden_f * hidden_f, axis=1, keepdims=True) + 1e-05)
        * norm_gain
    ).astype(jnp.bfloat16)
    logits = jnp.dot(normed, router, preferred_element_type=jnp.float32)
    expert_count = router.shape[1]
    expert_iota = lax.iota(jnp.int32, expert_count)
    picked = expert_ids[:, :, None] == expert_iota[None, None, :]
    chosen = jnp.sum(jnp.where(picked, logits[:, None, :], 0.0), axis=2)
    gates = jax.nn.sigmoid(chosen)
    gate_weights = gates / jnp.sum(gates, axis=1, keepdims=True)
    dense_gates = jnp.sum(jnp.where(picked, gate_weights[:, :, None], 0.0), axis=1)
    spread = ("seq", "head")
    all_rows = lax.all_gather(normed, spread, axis=0, tiled=True)
    all_gates = lax.all_gather(dense_gates, spread, axis=0, tiled=True)
    exp_dev = w_gate.shape[0]
    first = (lax.axis_index("seq") * lax.axis_size("head") + lax.axis_index("head")) * exp_dev
    partial = 0.0
    for own in range(exp_dev):
        gate = jnp.sum(jnp.where(expert_iota[None, :] == first + own, all_gates, 0.0), axis=1)
        partial = partial + run_expert(all_rows, gate, w_gate[own], w_up[own], w_down[own])
    expert_sum = lax.psum_scatter(
        partial.astype(jnp.bfloat16), spread, scatter_dimension=0, tiled=True
    )
    return (hidden, expert_sum)


def solution(mesh):
    placed = (
        P(("groups", "seq"), "head"),
        P(("groups", "seq"), "head"),
        P(("groups", "seq"), "head"),
        P(("groups", "seq")),
        P("head", None, None),
        P("head"),
        P(("groups", "seq", "head"), None),
        P("head", None),
        P(),
        P(),
        P(("seq", "head"), None, None),
        P(("seq", "head"), None, None),
        P(("seq", "head"), None, None),
        P(("groups", "seq", "head"), None),
    )
    return jax.shard_map(
        shards,
        mesh=mesh,
        in_specs=placed,
        out_specs=(P(("groups", "seq", "head"), None), P(("groups", "seq", "head"), None)),
        check_vma=False,
    )
```

profile of v0, /device:TPU:0, one launch (start us, length us, event | category | flops | bytes accessed | tf_op | source)
XLA Modules:
  0.0 290.1 jit_solution(12551976899202699490)
XLA Ops:
  7.3 0.7 all-gather.3.cloned.1.call-update
  8.6 1.2 slice_dynamic-update-slice_fusion
  9.9 13.1 %all-reduce = s32[8]{0:T(128)S(1)} all-reduce(s32[8]{0:T(128)S(1)} %get-tuple-element.4), channel_id=1, replica_groups=mesh['groups'=2,'seq'=8,'head'=2] {'seq'}, use_global_device_ids=true, to_apply=%add | all-reduce | flops 8 | bytes 64
  22.9 0.6 fusion.43
  24.2 0.7 compare_convert_fusion.1
  24.9 1.1 fusion.12
  26.1 1.2 fusion.44
  27.3 3.4 %collective-permute-start = (bf16[8,256,128]{2,1,0:T(8,128)(2,1)}, bf16[8,256,128]{2,1,0:T(8,128)(2,1)S(1)}, u32[]{:S(2)}, u32[]{:S(2)}) collective-permute-start(bf16[8,256,128]{2,1,0:T(8,128)(2,1)} %get-tuple-element.8), channel_id=1, source_target_pairs={{0,2},{2,4},{4,6},{6,8},{8,10},{10,12},{12,14},{1,3},{3,5},{5,7},{... | collective-permute-start | bytes 1572872 | tf_op jit(solution)/shard_map/ppermute | solution.py:24
  31.4 7.9 %collective-permute-done = bf16[8,256,128]{2,1,0:T(8,128)(2,1)S(1)} collective-permute-done((bf16[8,256,128]{2,1,0:T(8,128)(2,1)}, bf16[8,256,128]{2,1,0:T(8,128)(2,1)S(1)}, u32[]{:S(2)}, u32[]{:S(2)}) %collective-permute-start) | collective-permute-done | bytes 524320 | tf_op jit(solution)/shard_map/ppermute | solution.py:24
  39.3 0.9 fusion.18
  40.2 4.4 %collective-permute-start.1 = (bf16[8,256,128]{2,1,0:T(8,128)(2,1)}, bf16[8,256,128]{2,1,0:T(8,128)(2,1)S(1)}, u32[]{:S(2)}, u32[]{:S(2)}) collective-permute-start(bf16[8,256,128]{2,1,0:T(8,128)(2,1)} %fusion.18), channel_id=1, source_target_pairs={{0,4},{2,6},{4,8},{6,10},{8,12},{10,14},{1,5},{3,7},{5,9},{7,11},{... | collective-permute-start | bytes 1572872 | tf_op jit(solution)/shard_map/ppermute | solution.py:24
  45.4 2.2 fusion.9
  47.6 5.0 %collective-permute-done.1 = bf16[8,256,128]{2,1,0:T(8,128)(2,1)S(1)} collective-permute-done((bf16[8,256,128]{2,1,0:T(8,128)(2,1)}, bf16[8,256,128]{2,1,0:T(8,128)(2,1)S(1)}, u32[]{:S(2)}, u32[]{:S(2)}) %collective-permute-start.1) | collective-permute-done | bytes 524320 | tf_op jit(solution)/shard_map/ppermute | solution.py:24
  52.6 1.4 fusion.16
  54.0 2.5 multiply_reduce_fusion
  57.0 4.2 %all_to_all.16 = bf16[2,128,1024]{1,2,0:T(8,128)(2,1)S(1)} all-to-all(bf16[2,128,1024]{1,2,0:T(8,128)(2,1)S(1)} %copy.47), channel_id=1, replica_groups=mesh['groups'=2,'seq'=8,'head'=2] {'head'}, dimensions={0} | all-to-all | bytes 1048576 | tf_op jit(solution)/shard_map/all_to_all | solution.py:104
  61.2 4.8 %fusion.20 = (f32[128]{0:T(128)S(1)}, bf16[128,2048]{1,0:T(8,128)(2,1)S(1)}) fusion(bf16[128,2048]{0,1:T(8,128)(2,1)S(1)} %bitcast.71, bf16[2048,2048]{1,0:T(8,128)(2,1)} %all-gather.3.cloned.1.call-done, bf16[128,2048]{1,0:T(8,128)(2,1)S(1)} %copy-done.3), kind=kOutput, calls=%fused_computation.32 | convolution fusion | flops 1075314560 | bytes 9961984 | tf_op jit(solution)/shard_map/dot_general | solution.py:105
  66.0 1.0 fusion.22
  67.1 1.3 fusion.45
  68.5 20.6 %all_gather.15 = f32[2048,16]{0,1:T(8,128)S(1)} all-gather(f32[128,16]{0,1:T(8,128)S(1)} %select_reduce_fusion.1), channel_id=1, replica_groups=mesh['groups'=2,'seq'=8,'head'=2] {'seq','head'}, dimensions={0}, use_global_device_ids=true | all-gather | bytes 139264 | tf_op jit(solution)/shard_map/all_gather | solution.py:127
  89.2 51.7 %all-gather.5.cloned.1.call-done = bf16[2048,2048]{1,0:T(8,128)(2,1)} async-done(((bf16[128,2048]{1,0:T(8,128)(2,1)}), bf16[2048,2048]{1,0:T(8,128)(2,1)}) %all-gather.5.cloned.1.call-update) | async-done | bytes 8388624 | tf_op jit(solution)/shard_map/all_gather | solution.py:126
  140.9 14.4 %fusion.3 = f32[2048,1024]{1,0:T(8,128)} fusion(bf16[2048,2048]{1,0:T(8,128)(2,1)} %all-gather.5.cloned.1.call-done, bf16[1,2048,1024]{2,1,0:T(8,128)(2,1)} %param.24), kind=kOutput, calls=%fused_computation.8 | convolution fusion | flops 8589934592 | bytes 20971520 | tf_op jit(solution)/shard_map/dot_general | solution.py:45
  155.3 26.0 %multiply_convert_fusion = bf16[2048,2048]{1,0:T(8,128)(2,1)} fusion(f32[2048]{0:T(1024)S(1)} %select_reduce_fusion, f32[2048,1024]{1,0:T(8,128)} %fusion.3, bf16[2048,2048]{1,0:T(8,128)(2,1)} %all-gather.5.cloned.1.call-done, bf16[1,1024,2048]{2,1,0:T(8,128)(2,1)} %param.26, bf16[1,2048,1024]{2,1,0:T(8,128)(2,1)} %param.25), kind=kOutput, calls=%fused_computation | convolution fusion | flops 17200840704 | bytes 33562624 | tf_op jit(solution)/shard_map/dot_general | solution.py:48
  181.3 102.2 %reduce-scatter.2.cloned.1.call-done = bf16[128,2048]{1,0:T(8,128)(2,1)} async-done(((bf16[2048,2048]{1,0:T(8,128)(2,1)}), bf16[128,2048]{1,0:T(8,128)(2,1)}) %reduce-scatter.2.cloned.1.call-update) | async-done | bytes 524304 | tf_op jit(solution)/shard_map/reduce_scatter | solution.py:134
  (44 shorter events, 1.5 us)
Async XLA Ops:
  7.2 17.7 %copy-start = (bf16[8,128,256]{2,1,0:T(8,128)(2,1)S(1)}, bf16[8,128,256]{2,1,0:T(8,128)(2,1)}, u32[]{:S(2)}) copy-start(bf16[8,128,256]{2,1,0:T(8,128)(2,1)} %param.18) | copy-start | bytes 1572868
  7.2 0.8 copy-start.11
  7.2 1.4 copy-start.7
  7.2 17.7 %copy-start.10 = (bf16[256,1024]{1,0:T(8,128)(2,1)S(1)}, bf16[256,1024]{1,0:T(8,128)(2,1)}, u32[]{:S(2)}) copy-start(bf16[256,1024]{1,0:T(8,128)(2,1)} %param.15) | copy-start | bytes 1572868
  7.2 18.8 %copy-start.4 = (bf16[256,1024]{1,0:T(8,128)(2,1)S(1)}, bf16[256,1024]{1,0:T(8,128)(2,1)}, u32[]{:S(2)}) copy-start(bf16[256,1024]{1,0:T(8,128)(2,1)} %param.16) | copy-start | bytes 1572868
  7.2 53.9 %all-gather.3.cloned.1.call-start = ((), (), s32[]{:S(2)}) async-start(), calls=%async_computation.2 | async-start | bytes 12582912 | tf_op jit(solution)/shard_map/all_gather | solution.py:107
  8.0 133.0 %all-gather.5.cloned.1.call-start = ((), (), s32[]{:S(2)}) async-start(), calls=%async_computation.3 | async-start | bytes 8912896 | tf_op jit(solution)/shard_map/all_gather | solution.py:126
  27.3 12.0 %collective-permute-start = (bf16[8,256,128]{2,1,0:T(8,128)(2,1)}, bf16[8,256,128]{2,1,0:T(8,128)(2,1)S(1)}, u32[]{:S(2)}, u32[]{:S(2)}) collective-permute-start(bf16[8,256,128]{2,1,0:T(8,128)(2,1)} %get-tuple-element.8), channel_id=1, source_target_pairs={{0,2},{2,4},{4,6},{6,8},{8,10},{10,12},{12,14},{1,3},{3,5},{5,7},{... | collective-permute-start | bytes 1572872 | tf_op jit(solution)/shard_map/ppermute | solution.py:24
  40.2 12.3 %collective-permute-start.1 = (bf16[8,256,128]{2,1,0:T(8,128)(2,1)}, bf16[8,256,128]{2,1,0:T(8,128)(2,1)S(1)}, u32[]{:S(2)}, u32[]{:S(2)}) collective-permute-start(bf16[8,256,128]{2,1,0:T(8,128)(2,1)} %fusion.18), channel_id=1, source_target_pairs={{0,4},{2,6},{4,8},{6,10},{8,12},{10,14},{1,5},{3,7},{5,9},{7,11},{... | collective-permute-start | bytes 1572872 | tf_op jit(solution)/shard_map/ppermute | solution.py:24
  47.5 5.0 %copy-start.2 = (bf16[256,8,256]{0,2,1:T(8,128)(2,1)}, bf16[256,8,256]{0,2,1:T(8,128)(2,1)S(1)}, u32[]{:S(2)}) copy-start(bf16[256,8,256]{0,2,1:T(8,128)(2,1)S(1)} %fusion.9) | copy-start | bytes 3145732
  47.5 9.0 %copy-start.9 = (f32[1024]{0:T(1024)S(1)}, f32[1024]{0:T(1024)}, u32[]{:S(2)}) copy-start(f32[1024]{0:T(1024)} %param.19) | copy-start | bytes 12292
  54.0 7.1 %copy-start.3 = (bf16[128,2048]{1,0:T(8,128)(2,1)S(1)}, bf16[128,2048]{1,0:T(8,128)(2,1)}, u32[]{:S(2)}) copy-start(bf16[128,2048]{1,0:T(8,128)(2,1)} %param.20) | copy-start | bytes 1572868
  61.1 4.9 %copy-start.8 = (f32[2048]{0:T(1024)S(1)}, f32[2048]{0:T(1024)}, u32[]{:S(2)}) copy-start(f32[2048]{0:T(1024)} %param.22) | copy-start | bytes 24580
  61.1 5.9 %copy-start.5 = (bf16[2048,16]{0,1:T(8,128)(2,1)S(1)}, bf16[2048,16]{0,1:T(8,128)(2,1)}, u32[]{:S(2)}) copy-start(bf16[2048,16]{0,1:T(8,128)(2,1)} %param.23) | copy-start | bytes 196612
  61.1 7.2 %copy-start.6 = (s32[128,8]{0,1:T(8,128)S(1)}, s32[128,8]{0,1:T(8,128)}, u32[]{:S(2)}) copy-start(s32[128,8]{0,1:T(8,128)} %param.27) | copy-start | bytes 12292
  66.0 89.4 %copy-start.1 = (bf16[128,2048]{1,0:T(8,128)(2,1)}, bf16[128,2048]{1,0:T(8,128)(2,1)S(1)}, u32[]{:S(2)}) copy-start(bf16[128,2048]{1,0:T(8,128)(2,1)S(1)} %get-tuple-element.13) | copy-start | bytes 1572868
  67.0 216.5 %reduce-scatter.2.cloned.1.call-start = ((), (), s32[]{:S(2)}) async-start(), calls=%async_computation.4 | async-start | bytes 8912896 | tf_op jit(solution)/shard_map/reduce_scatter | solution.py:134
Sparse Core Ops, SparseCore 0:
  9.6 22.5 all-gather.2
  67.1 73.7 all-gather.4
  181.5 102.0 reduce-scatter.1
where the time goes:
time: 290 us
  waiting for transfers between devices  168 us (58%)
  matrix products  54.9 us (19%)
  blocking collectives  37.9 us (13%)
  between operations  16 us (6%)
  starting transfers between devices  7.95 us (3%)
  other arithmetic  3.09 us (1%)
    reduce_scatter x1, waiting for transfers between devices, shards(): lax.psum_scatter(partial.astype(jnp.bfloat16), spread, scatter_dimension=...  102 us
    all_gather x1, waiting for transfers between devices, shards(): all_rows = lax.all_gather(normed, spread, axis=0, tiled=True)  51.7 us
    dot_general x1, matrix products, run_expert(): answer = jnp.dot(activated, w_down, preferred_element_type=jnp.float32)  26 us
    all_gather x1, blocking collectives, shards(): all_gates = lax.all_gather(dense_gates, spread, axis=0, tiled=True)  20.6 us
    dot_general x1, matrix products, run_expert(): gate_pre = jnp.dot(rows, w_gate, preferred_element_type=jnp.float32)  14.4 us
    unnamed x1, blocking collectives  13.1 us
    ppermute x2, waiting for transfers between devices, carried_in(): lax.ppermute(window.astype(jnp.bfloat16), 'seq', [(i, i + span) for i in...  12.9 us
    ppermute x2, starting transfers between devices, carried_in(): lax.ppermute(window.astype(jnp.bfloat16), 'seq', [(i, i + span) for i in...  7.83 us
  transfers between devices with their start and end apart: 5, of which 4 were waited for; matrix products, arithmetic and copies ran while one was open for 5% of the time, Pallas kernels for 0%

commit v1 on v0

--- a/solution.py
+++ b/solution.py
@@ -123,8 +123,11 @@
     gate_weights = gates / jnp.sum(gates, axis=1, keepdims=True)
     dense_gates = jnp.sum(jnp.where(picked, gate_weights[:, :, None], 0.0), axis=1)
     spread = ("seq", "head")
-    all_rows = lax.all_gather(normed, spread, axis=0, tiled=True)
-    all_gates = lax.all_gather(dense_gates, spread, axis=0, tiled=True)
+    all_rows, all_gates = jnp.split(
+        lax.all_gather(jnp.concatenate([normed, dense_gates], axis=1), spread, axis=0, tiled=True),
+        [normed.shape[1]],
+        axis=1,
+    )
     exp_dev = w_gate.shape[0]
     first = (lax.axis_index("seq") * lax.axis_size("head") + lax.axis_index("head")) * exp_dev
     partial = 0.0

time: 290 us -> 315 us (1.086)
  waiting for transfers between devices: 168 us -> 210 us
  blocking collectives: 37.9 us -> 17.2 us
    all_gather x1, waiting for transfers between devices: 51.7 us -> 93 us  [shards(): lax.all_gather(jnp.concatenate([normed, dense_gates], axis=1), spread, ax...]
    all_gather x1 -> x0, blocking collectives: 20.6 us -> none  [shards(): all_gates = lax.all_gather(dense_gates, spread, axis=0, tiled=True)]
  transfers between devices with their start and end apart: 5 -> 5, of which waited for: 4 -> 4; matrix products, arithmetic and copies ran while one was open for 5% -> 4% of each run, Pallas kernels for 0% -> 0%
where the time goes in v1:
time: 315 us; the launch traced here: 314 us
  waiting for transfers between devices  210 us (67%)
  matrix products  55 us (17%)
  blocking collectives  17.2 us (5%)
  between operations  16 us (5%)
  starting transfers between devices  8.13 us (3%)
  other arithmetic  4.86 us (2%)
    reduce_scatter x1, waiting for transfers between devices, shards(): lax.psum_scatter(partial.astype(jnp.bfloat16), spread, scatter_dimension=...  104 us
    all_gather x1, waiting for transfers between devices, shards(): lax.all_gather(jnp.concatenate([normed, dense_gates], axis=1), spread, ax...  93 us
    dot_general x1, matrix products, run_expert(): answer = jnp.dot(activated, w_down, preferred_element_type=jnp.float32)  25.9 us
    dot_general x1, matrix products, run_expert(): gate_pre = jnp.dot(rows, w_gate, preferred_element_type=jnp.float32)  15.6 us
    unnamed x1, blocking collectives  13.1 us
    ppermute x2, waiting for transfers between devices, carried_in(): lax.ppermute(window.astype(jnp.bfloat16), 'seq', [(i, i + span) for i in...  12.9 us
    ppermute x2, starting transfers between devices, carried_in(): lax.ppermute(window.astype(jnp.bfloat16), 'seq', [(i, i + span) for i in...  7.83 us
  transfers between devices with their start and end apart: 5, of which 4 were waited for; matrix products, arithmetic and copies ran while one was open for 4% of the time, Pallas kernels for 0%

profile of v1, /device:TPU:0, one launch (start us, length us, event | category | flops | bytes accessed | tf_op | source)
XLA Modules:
  0.0 314.3 jit_solution(13112510402077097500)
XLA Ops:
  7.3 0.7 all-gather.3.cloned.1.call-update
  8.0 0.6 dynamic-slice
  8.6 1.2 slice_dynamic-update-slice_fusion
  9.9 13.1 %all-reduce = s32[8]{0:T(128)S(1)} all-reduce(s32[8]{0:T(128)S(1)} %get-tuple-element.4), channel_id=1, replica_groups=mesh['groups'=2,'seq'=8,'head'=2] {'seq'}, use_global_device_ids=true, to_apply=%add | all-reduce | flops 8 | bytes 64
  22.9 0.6 fusion.54
  24.2 0.7 compare_convert_fusion.1
  24.9 1.1 fusion.19
  26.0 1.2 fusion.55
  27.2 3.4 %collective-permute-start = (bf16[8,256,128]{2,1,0:T(8,128)(2,1)}, bf16[8,256,128]{2,1,0:T(8,128)(2,1)S(1)}, u32[]{:S(2)}, u32[]{:S(2)}) collective-permute-start(bf16[8,256,128]{2,1,0:T(8,128)(2,1)} %get-tuple-element.8), channel_id=1, source_target_pairs={{0,2},{2,4},{4,6},{6,8},{8,10},{10,12},{12,14},{1,3},{3,5},{5,7},{... | collective-permute-start | bytes 1572872 | tf_op jit(solution)/shard_map/ppermute | solution.py:24
  31.4 7.9 %collective-permute-done = bf16[8,256,128]{2,1,0:T(8,128)(2,1)S(1)} collective-permute-done((bf16[8,256,128]{2,1,0:T(8,128)(2,1)}, bf16[8,256,128]{2,1,0:T(8,128)(2,1)S(1)}, u32[]{:S(2)}, u32[]{:S(2)}) %collective-permute-start) | collective-permute-done | bytes 524320 | tf_op jit(solution)/shard_map/ppermute | solution.py:24
  39.3 0.9 fusion.25
  40.2 4.4 %collective-permute-start.1 = (bf16[8,256,128]{2,1,0:T(8,128)(2,1)}, bf16[8,256,128]{2,1,0:T(8,128)(2,1)S(1)}, u32[]{:S(2)}, u32[]{:S(2)}) collective-permute-start(bf16[8,256,128]{2,1,0:T(8,128)(2,1)} %fusion.25), channel_id=1, source_target_pairs={{0,4},{2,6},{4,8},{6,10},{8,12},{10,14},{1,5},{3,7},{5,9},{7,11},{... | collective-permute-start | bytes 1572872 | tf_op jit(solution)/shard_map/ppermute | solution.py:24
  45.3 2.2 fusion.16
  47.5 5.0 %collective-permute-done.1 = bf16[8,256,128]{2,1,0:T(8,128)(2,1)S(1)} collective-permute-done((bf16[8,256,128]{2,1,0:T(8,128)(2,1)}, bf16[8,256,128]{2,1,0:T(8,128)(2,1)S(1)}, u32[]{:S(2)}, u32[]{:S(2)}) %collective-permute-start.1) | collective-permute-done | bytes 524320 | tf_op jit(solution)/shard_map/ppermute | solution.py:24
  52.5 1.4 fusion.23
  54.0 2.5 multiply_reduce_fusion
  56.9 4.2 %all_to_all.16 = bf16[2,128,1024]{1,2,0:T(8,128)(2,1)S(1)} all-to-all(bf16[2,128,1024]{1,2,0:T(8,128)(2,1)S(1)} %copy.47), channel_id=1, replica_groups=mesh['groups'=2,'seq'=8,'head'=2] {'head'}, dimensions={0} | all-to-all | bytes 1048576 | tf_op jit(solution)/shard_map/all_to_all | solution.py:104
  61.1 4.8 %fusion.27 = (f32[128]{0:T(128)S(1)}, bf16[128,2048]{1,0:T(8,128)(2,1)S(1)}) fusion(bf16[128,2048]{0,1:T(8,128)(2,1)S(1)} %bitcast.68, bf16[2048,2048]{1,0:T(8,128)(2,1)} %all-gather.3.cloned.1.call-done, bf16[128,2048]{1,0:T(8,128)(2,1)S(1)} %copy-done.4), kind=kOutput, calls=%fused_computation.36 | convolution fusion | flops 1075314560 | bytes 9961984 | tf_op jit(solution)/shard_map/dot_general | solution.py:105
  66.7 1.1 pad_maximum_fusion
  68.1 93.0 %all-gather.5.cloned.1.call-done = f32[2048,2064]{1,0:T(8,128)} async-done(((f32[128,2064]{1,0:T(8,128)}), f32[2048,2064]{1,0:T(8,128)}) %all-gather.5.cloned.1.call-update) | async-done | bytes 16908304 | tf_op jit(solution)/shard_map/all_gather | solution.py:127
  161.0 1.6 fusion.30
  162.6 15.6 %fusion.2 = f32[2048,1024]{1,0:T(8,128)} fusion(f32[2048,2064]{1,0:T(8,128)} %all-gather.5.cloned.1.call-done, bf16[1,2048,1024]{2,1,0:T(8,128)(2,1)} %param.24), kind=kOutput, calls=%fused_computation.3 | convolution fusion | flops 8589934592 | bytes 20971520 | tf_op jit(solution)/shard_map/dot_general | solution.py:45
  178.2 25.9 %multiply_convert_fusion = bf16[2048,2048]{1,0:T(8,128)(2,1)} fusion(f32[2048]{0:T(1024)S(1)} %fusion.30, f32[2048,1024]{1,0:T(8,128)} %fusion.2, f32[2048,2064]{1,0:T(8,128)} %all-gather.5.cloned.1.call-done, bf16[1,1024,2048]{2,1,0:T(8,128)(2,1)} %param.26, bf16[1,2048,1024]{2,1,0:T(8,128)(2,1)} %param.25), kind=kOutput, calls=%fused_computation | convolution fusion | flops 17200840704 | bytes 33562624 | tf_op jit(solution)/shard_map/dot_general | solution.py:48
  204.1 103.6 %reduce-scatter.2.cloned.1.call-done = bf16[128,2048]{1,0:T(8,128)(2,1)} async-done(((bf16[2048,2048]{1,0:T(8,128)(2,1)}), bf16[128,2048]{1,0:T(8,128)(2,1)}) %reduce-scatter.2.cloned.1.call-update) | async-done | bytes 524304 | tf_op jit(solution)/shard_map/reduce_scatter | solution.py:137
  (47 shorter events, 1.6 us)
Async XLA Ops:
  7.2 17.7 %copy-start = (bf16[8,128,256]{2,1,0:T(8,128)(2,1)S(1)}, bf16[8,128,256]{2,1,0:T(8,128)(2,1)}, u32[]{:S(2)}) copy-start(bf16[8,128,256]{2,1,0:T(8,128)(2,1)} %param.18) | copy-start | bytes 1572868
  7.2 0.8 copy-start.12
  7.2 1.4 copy-start.7
  7.2 17.7 %copy-start.10 = (bf16[256,1024]{1,0:T(8,128)(2,1)S(1)}, bf16[256,1024]{1,0:T(8,128)(2,1)}, u32[]{:S(2)}) copy-start(bf16[256,1024]{1,0:T(8,128)(2,1)} %param.15) | copy-start | bytes 1572868
  7.2 18.8 %copy-start.5 = (bf16[256,1024]{1,0:T(8,128)(2,1)S(1)}, bf16[256,1024]{1,0:T(8,128)(2,1)}, u32[]{:S(2)}) copy-start(bf16[256,1024]{1,0:T(8,128)(2,1)} %param.16) | copy-start | bytes 1572868
  7.2 53.9 %all-gather.3.cloned.1.call-start = ((), (), s32[]{:S(2)}) async-start(), calls=%async_computation.2 | async-start | bytes 12582912 | tf_op jit(solution)/shard_map/all_gather | solution.py:107
  8.0 153.1 %all-gather.5.cloned.1.call-start = ((), (), s32[]{:S(2)}) async-start(), calls=%async_computation.3 | async-start | bytes 18939904 | tf_op jit(solution)/shard_map/all_gather | solution.py:127
  27.2 12.0 %collective-permute-start = (bf16[8,256,128]{2,1,0:T(8,128)(2,1)}, bf16[8,256,128]{2,1,0:T(8,128)(2,1)S(1)}, u32[]{:S(2)}, u32[]{:S(2)}) collective-permute-start(bf16[8,256,128]{2,1,0:T(8,128)(2,1)} %get-tuple-element.8), channel_id=1, source_target_pairs={{0,2},{2,4},{4,6},{6,8},{8,10},{10,12},{12,14},{1,3},{3,5},{5,7},{... | collective-permute-start | bytes 1572872 | tf_op jit(solution)/shard_map/ppermute | solution.py:24
  40.2 12.3 %collective-permute-start.1 = (bf16[8,256,128]{2,1,0:T(8,128)(2,1)}, bf16[8,256,128]{2,1,0:T(8,128)(2,1)S(1)}, u32[]{:S(2)}, u32[]{:S(2)}) collective-permute-start(bf16[8,256,128]{2,1,0:T(8,128)(2,1)} %fusion.25), channel_id=1, source_target_pairs={{0,4},{2,6},{4,8},{6,10},{8,12},{10,14},{1,5},{3,7},{5,9},{7,11},{... | collective-permute-start | bytes 1572872 | tf_op jit(solution)/shard_map/ppermute | solution.py:24
  47.5 5.0 %copy-start.3 = (bf16[256,8,256]{0,2,1:T(8,128)(2,1)}, bf16[256,8,256]{0,2,1:T(8,128)(2,1)S(1)}, u32[]{:S(2)}) copy-start(bf16[256,8,256]{0,2,1:T(8,128)(2,1)S(1)} %fusion.16) | copy-start | bytes 3145732
  47.5 9.0 %copy-start.9 = (f32[1024]{0:T(1024)S(1)}, f32[1024]{0:T(1024)}, u32[]{:S(2)}) copy-start(f32[1024]{0:T(1024)} %param.19) | copy-start | bytes 12292
  54.0 7.1 %copy-start.4 = (bf16[128,2048]{1,0:T(8,128)(2,1)S(1)}, bf16[128,2048]{1,0:T(8,128)(2,1)}, u32[]{:S(2)}) copy-start(bf16[128,2048]{1,0:T(8,128)(2,1)} %param.20) | copy-start | bytes 1572868
  61.1 4.8 %copy-start.8 = (f32[2048]{0:T(1024)S(1)}, f32[2048]{0:T(1024)}, u32[]{:S(2)}) copy-start(f32[2048]{0:T(1024)} %param.22) | copy-start | bytes 24580
  61.1 5.0 %copy-start.11 = (bf16[2048,16]{0,1:T(8,128)(2,1)S(1)}, bf16[2048,16]{0,1:T(8,128)(2,1)}, u32[]{:S(2)}) copy-start(bf16[2048,16]{0,1:T(8,128)(2,1)} %param.23) | copy-start | bytes 196612
  61.1 5.4 %copy-start.6 = (s32[128,8]{0,1:T(8,128)S(1)}, s32[128,8]{0,1:T(8,128)}, u32[]{:S(2)}) copy-start(s32[128,8]{0,1:T(8,128)} %param.27) | copy-start | bytes 12292
  65.9 112.3 %copy-start.2 = (bf16[128,2048]{1,0:T(8,128)(2,1)}, bf16[128,2048]{1,0:T(8,128)(2,1)S(1)}, u32[]{:S(2)}) copy-start(bf16[128,2048]{1,0:T(8,128)(2,1)S(1)} %get-tuple-element.13) | copy-start | bytes 1572868
  67.8 239.9 %reduce-scatter.2.cloned.1.call-start = ((), (), s32[]{:S(2)}) async-start(), calls=%async_computation.4 | async-start | bytes 8912896 | tf_op jit(solution)/shard_map/reduce_scatter | solution.py:137
  204.1 103.6 %copy-start.1 = (bf16[8,128,256]{2,1,0:T(8,128)(2,1)S(1)}, bf16[8,128,256]{2,1,0:T(8,128)(2,1)}, u32[]{:S(2)}) copy-start(bf16[8,128,256]{2,1,0:T(8,128)(2,1)} %param.18) | copy-start | bytes 1572868
Sparse Core Ops, SparseCore 0:
  9.6 22.5 all-gather.2
  67.9 93.0 all-gather.4
  204.2 103.4 reduce-scatter.1
